TPU v7x, 128 devices: a whole 4x4x4 slice. The times are simulated.
128 devices in a mesh: dev: 32 (over z, x, core), rep: 4 (over y).
Axes of the slice: x: 4, y: 4, z: 4, core: 2. Of those that a mesh axis runs over, the one named last changes fastest.
Arguments:
- activations: bfloat16 [4, 256, 64, 2048], P('rep', 'dev'), may hold values from -6 to 6
- out_grads: bfloat16 [4, 256, 64, 1024], P('rep', 'dev'), may hold values from -6 to 6
- inverse: float32 [32, 2048, 2048], P('dev'), may hold values from -4 to 11, as said below
Outputs:
- whitened: float32 [4, 256, 65536], P('rep', 'dev')
- leverage: float32 [4, 256], P('rep', 'dev')
- new_inverse: float32 [32, 2048, 2048], P('dev', 'rep')
Inputs may be any that keep to these rules, and one draw needn't show every extreme that they name: Each 2048 x 2048 matrix of inverse is symmetric positive definite.
All inputs are finite; a program needn't handle non-finite values.
Results may differ from a plain program's by a relative error of at most 0.0003.
Values sent between devices are 32-bit elements; how exact they have to be, the bound alone decides.
No kernel may reach another device: no remote copies, remote signals or barrier semaphores. Data moves between devices by JAX's collectives and lax.ppermute only.
A program may use at most 128 MiB of HBM per device.

v0:
```python
import jax
import jax.numpy as jnp
from jax import lax
from jax.sharding import PartitionSpec as P

KI = 64
KO = 32


def body(activations, out_grads, inverse):
    num_dev = lax.axis_size("dev")
    num_rep = lax.axis_size("rep")
    examples = activations.shape[1]
    tokens = activations.shape[2]
    feat_width = KI * KO
    group_rows = examples * num_dev
    acts_four = activations.reshape(examples, tokens, num_dev, KI)
    grads_four = out_grads.reshape(examples, tokens, num_dev, KO)
    features = jnp.einsum(
        "etmo,etmi->emoi", grads_four, acts_four, preferred_element_type=jnp.float32
    )
    features = features.reshape(examples, num_dev, feat_width) * tokens ** (-0.5)
    moved = lax.all_to_all(features, "dev", split_axis=1, concat_axis=0, tiled=True)
    own_rows = moved[:, 0, :]
    module_inverse = inverse[0]
    whitened = jnp.dot(own_rows, module_inverse, precision=lax.Precision.HIGHEST)
    lev_terms = jnp.sum(own_rows * whitened, axis=1)
    lev_send = lax.psum(lev_terms, "dev") / (num_dev * feat_width)
    all_rows, all_white, all_lev = (
        lax.all_gather(own_rows, "rep", axis=0, tiled=True),
        lax.all_gather(whitened, "rep", axis=0, tiled=True),
        lax.all_gather(lev_send, "rep", axis=0, tiled=True),
    )
    damping = 1.0 + feat_width * all_lev
    capacitance = jnp.dot(all_rows, all_white.T, precision=lax.Precision.HIGHEST) + jnp.diag(
        damping
    )
    cholesky_factor = jnp.linalg.cholesky(capacitance)
    row_count = feat_width // num_rep
    first_row = lax.axis_index("rep") * row_count
    white_block = lax.dynamic_slice_in_dim(all_white, first_row, row_count, 1)
    solved = jax.scipy.linalg.cho_solve((cholesky_factor, True), white_block)
    inverse_rows = lax.dynamic_slice_in_dim(module_inverse, first_row, row_count, 0)
    updated = inverse_rows - jnp.dot(solved.T, all_white, precision=lax.Precision.HIGHEST)
    returned = lax.all_to_all(
        whitened.reshape(num_dev, examples, 1, feat_width),
        "dev",
        split_axis=0,
        concat_axis=2,
        tiled=True,
    )
    whitened_out = returned.reshape(1, examples, num_dev * feat_width)
    lev_first = lax.axis_index("rep") * group_rows + lax.axis_index("dev") * examples
    lev_out = lax.dynamic_slice_in_dim(all_lev, lev_first, examples, 0).reshape(1, examples)
    return (whitened_out, lev_out, updated.reshape(1, row_count, feat_width))


def solution(mesh):
    in_specs = (P("rep", "dev", None, None), P("rep", "dev", None, None), P("dev", None, None))
    out_specs = (P("rep", "dev", None), P("rep", "dev"), P("dev", "rep", None))
    return jax.shard_map(body, mesh=mesh, in_specs=in_specs, out_specs=out_specs, check_vma=False)
```

profile of v0, /device:TPU:1, one launch (start us, length us, event | category | flops | bytes accessed | tf_op | source)
XLA Modules:
  0.0 655.6 jit_solution(12305604017612134976)
XLA Ops:
  7.2 2.0 copy.14
  9.2 7.1 %reshape.131 = bf16[8,64,32,64]{3,2,1,0:T(8,128)(2,1)} reshape(bf16[1,8,64,2048]{3,2,1,0:T(8,128)(2,1)} %param.3) | data formatting | bytes 4194304 | tf_op jit(solution)/shard_map/reshape | solution.py:17
  16.3 5.6 fusion.7
  21.9 3.6 mul.29
  25.6 1.2 copy.16
  26.8 37.5 %all_to_all.30 = f32[8,32,2048]{2,0,1:T(8,128)S(1)} all-to-all(f32[8,32,2048]{2,0,1:T(8,128)S(1)} %copy.16), channel_id=1, replica_groups=mesh['dev'=32,'rep'=4] {'dev'}, dimensions={1} | all-to-all | bytes 4194304 | tf_op jit(solution)/shard_map/all_to_all | solution.py:23
  64.3 18.8 %multiply_reduce_fusion = (f32[256]{0:T(256)S(1)}, f32[256,2048]{1,0:T(8,128)}) fusion(f32[8,32,2048]{2,0,1:T(8,128)S(1)} %all_to_all.30, f32[1,2048,2048]{2,1,0:T(8,128)} %param.5), kind=kOutput, calls=%fused_computation.16 | convolution fusion | flops 12885950464 | bytes 20972544 | tf_op jit(solution)/shard_map/dot_general | solution.py:26
  83.8 4.1 all-to-all-start.1
  88.0 81.7 %psum.7 = f32[256]{0:T(256)S(1)} all-reduce(f32[256]{0:T(256)S(1)} %get-tuple-element.60), channel_id=1, replica_groups=mesh['dev'=32,'rep'=4] {'dev'}, use_global_device_ids=true, to_apply=%region_1.0 | all-reduce | flops 256 | bytes 2048 | tf_op jit(solution)/shard_map/psum | solution.py:28
  169.7 8.2 %all-gather = f32[4,1,256]{2,1,0:T(1,128)S(1)} all-gather(f32[1,1,256]{2,1,0:T(1,128)S(1)} %bitcast.179), channel_id=1, replica_groups=mesh['dev'=32,'rep'=4] {'rep'}, dimensions={0}, use_global_device_ids=true | all-gather | bytes 5120 | tf_op jit(solution)/shard_map/all_gather | solution.py:32
  178.5 71.6 %all-gather.4.cloned.1.call-done = f32[1024,2048]{1,0:T(8,128)} async-done(((f32[256,2048]{1,0:T(8,128)}), f32[1024,2048]{1,0:T(8,128)}) %all-gather.4.cloned.1.call-update) | async-done | bytes 8388624 | tf_op jit(solution)/shard_map/all_gather | solution.py:30
  250.1 32.1 %fusion.106 = f32[1024,1024]{1,0:T(8,128)} fusion(f32[1024,2048]{1,0:T(8,128)} %all-gather.4.cloned.1.call-done, f32[1024,2048]{1,0:T(8,128)} %all-gather.6.cloned.1.call-done), kind=kOutput, calls=%fused_computation.229 | convolution fusion | flops 25769803776 | bytes 20971520 | tf_op jit(solution)/shard_map/dot_general | solution.py:35
  282.2 5.7 copy.18
  287.9 4.5 fusion.3
  292.5 2.0 copy-done.2
  294.4 11.7 %cholesky.222 = f32[128,128]{1,0:T(8,128)S(1)} custom-call(f32[128,128]{1,0:T(8,128)S(1)} %cholesky.577), custom_call_target="Cholesky" | custom-call | tf_op jit(solution)/shard_map/jit(cholesky)/cholesky | solution.py:38
  306.2 2.5 cholesky.254
  308.7 9.8 %custom-call.66 = f32[1,128,128]{1,2,0:T(8,128)S(1)} custom-call(f32[1,128,128]{2,1,0:T(8,128)S(1)} %get-tuple-element.59), custom_call_target="InvertDiagBlocksLowerTriangular" | custom-call | tf_op jit(solution)/shard_map/jit(cholesky)/cholesky | solution.py:38
  318.6 2.3 constant_dynamic-update-slice_fusion.48
  320.9 1.5 convolution_subtract_fusion
  322.4 11.8 %cholesky.243 = f32[128,128]{1,0:T(8,128)S(1)} custom-call(f32[128,128]{1,0:T(8,128)S(1)} %cholesky.581), custom_call_target="Cholesky" | custom-call | tf_op jit(solution)/shard_map/jit(cholesky)/cholesky | solution.py:38
  334.9 9.8 %custom-call.67 = f32[1,128,128]{1,2,0:T(8,128)S(1)} custom-call(f32[1,128,128]{2,1,0:T(8,128)S(1)} %get-tuple-element.56), custom_call_target="InvertDiagBlocksLowerTriangular" | custom-call | tf_op jit(solution)/shard_map/jit(cholesky)/cholesky | solution.py:38
  344.7 1.2 convolution_dynamic-update-slice_fusion
  345.9 2.1 convolution_subtract_fusion.1
  348.1 11.7 %cholesky.466 = f32[128,128]{1,0:T(8,128)S(1)} custom-call(f32[128,128]{1,0:T(8,128)S(1)} %cholesky.586), custom_call_target="Cholesky" | custom-call | tf_op jit(solution)/shard_map/jit(cholesky)/cholesky | solution.py:38
  360.4 9.8 %custom-call.68 = f32[1,128,128]{1,2,0:T(8,128)S(1)} custom-call(f32[1,128,128]{2,1,0:T(8,128)S(1)} %get-tuple-element.53), custom_call_target="InvertDiagBlocksLowerTriangular" | custom-call | tf_op jit(solution)/shard_map/jit(cholesky)/cholesky | solution.py:38
  370.2 1.1 convolution_dynamic-update-slice_fusion.1
  371.4 2.3 convolution_subtract_fusion.2
  373.7 11.9 %cholesky.485 = f32[128,128]{1,0:T(8,128)S(1)} custom-call(f32[128,128]{1,0:T(8,128)S(1)} %cholesky.591), custom_call_target="Cholesky" | custom-call | tf_op jit(solution)/shard_map/jit(cholesky)/cholesky | solution.py:38
  386.3 9.8 %custom-call.69 = f32[1,128,128]{1,2,0:T(8,128)S(1)} custom-call(f32[1,128,128]{2,1,0:T(8,128)S(1)} %get-tuple-element.50), custom_call_target="InvertDiagBlocksLowerTriangular" | custom-call | tf_op jit(solution)/shard_map/jit(cholesky)/cholesky | solution.py:38
  397.2 2.3 convolution_subtract_fusion.17
  399.5 11.7 %cholesky.504 = f32[128,128]{1,0:T(8,128)S(1)} custom-call(f32[128,128]{1,0:T(8,128)S(1)} %cholesky.596), custom_call_target="Cholesky" | custom-call | tf_op jit(solution)/shard_map/jit(cholesky)/cholesky | solution.py:38
  411.9 10.2 %custom-call.70 = f32[1,128,128]{1,2,0:T(8,128)S(1)} custom-call(f32[1,128,128]{2,1,0:T(8,128)S(1)} %get-tuple-element.47), custom_call_target="InvertDiagBlocksLowerTriangular" | custom-call | tf_op jit(solution)/shard_map/jit(cholesky)/cholesky | solution.py:38
  423.0 2.3 convolution_subtract_fusion.18
  425.3 11.7 %cholesky.524 = f32[128,128]{1,0:T(8,128)S(1)} custom-call(f32[128,128]{1,0:T(8,128)S(1)} %cholesky.601), custom_call_target="Cholesky" | custom-call | tf_op jit(solution)/shard_map/jit(cholesky)/cholesky | solution.py:38
  437.7 9.8 %custom-call.71 = f32[1,128,128]{1,2,0:T(8,128)S(1)} custom-call(f32[1,128,128]{2,1,0:T(8,128)S(1)} %get-tuple-element.44), custom_call_target="InvertDiagBlocksLowerTriangular" | custom-call | tf_op jit(solution)/shard_map/jit(cholesky)/cholesky | solution.py:38
  448.4 2.1 convolution_subtract_fusion.19
  450.5 11.9 %cholesky.544 = f32[128,128]{1,0:T(8,128)S(1)} custom-call(f32[128,128]{1,0:T(8,128)S(1)} %cholesky.606), custom_call_target="Cholesky" | custom-call | tf_op jit(solution)/shard_map/jit(cholesky)/cholesky | solution.py:38
  463.0 9.8 %custom-call.72 = f32[1,128,128]{1,2,0:T(8,128)S(1)} custom-call(f32[1,128,128]{2,1,0:T(8,128)S(1)} %get-tuple-element.41), custom_call_target="InvertDiagBlocksLowerTriangular" | custom-call | tf_op jit(solution)/shard_map/jit(cholesky)/cholesky | solution.py:38
  473.7 1.8 convolution_subtract_fusion.20
  475.5 11.7 %cholesky.562 = f32[128,128]{1,0:T(8,128)S(1)} custom-call(f32[128,128]{1,0:T(8,128)S(1)} %convolution_subtract_fusion.20), custom_call_target="Cholesky" | custom-call | tf_op jit(solution)/shard_map/jit(cholesky)/cholesky | solution.py:38
  497.2 4.9 select_select_fusion
  502.1 22.6 %while.1 = (s32[]{:T(128)}, f32[1024,1024]{1,0:T(8,128)}, s32[8,2]{0,1:T(2,128)S(1)}, f32[8,128,128]{2,1,0:T(8,128)S(1)}, s32[]{:T(128)}) while((s32[]{:T(128)}, f32[1024,1024]{1,0:T(8,128)}, s32[8,2]{0,1:T(2,128)S(1)}, f32[8,128,128]{2,1,0:T(8,128)S(1)}, s32[]{:T(128)}) %tuple.61), condition=%wide.while_cond, body=%wide.while_body.sunk | while | flops 2 | bytes 131189 | solution.py:42
  502.7 2.2 bitcast_dynamic-update-slice_fusion.2
  505.6 2.2 bitcast_dynamic-update-slice_fusion.2
  508.4 2.2 bitcast_dynamic-update-slice_fusion.2
  511.2 2.2 bitcast_dynamic-update-slice_fusion.2
  514.1 2.2 bitcast_dynamic-update-slice_fusion.2
  516.9 2.2 bitcast_dynamic-update-slice_fusion.2
  519.7 2.2 bitcast_dynamic-update-slice_fusion.2
  522.5 2.1 bitcast_dynamic-update-slice_fusion.2
  524.7 78.8 %custom-call.73 = f32[8,128,128]{1,2,0:T(8,128)S(1)} custom-call(f32[8,128,128]{2,1,0:T(8,128)S(1)} %get-tuple-element.10), custom_call_target="InvertDiagBlocksLowerTriangular" | custom-call | tf_op jit(solution)/shard_map/jit(_cho_solve)/triangular_solve | solution.py:42
  603.5 1.4 constant_dynamic-update-slice_fusion.10
  605.0 1.5 convolution_subtract_fusion.10
  606.9 1.5 convolution_subtract_fusion.9
  608.9 1.6 convolution_subtract_fusion.14
  610.9 1.7 convolution_subtract_fusion.16
  613.1 1.9 convolution_subtract_fusion.8
  615.4 2.0 convolution_subtract_fusion.13
  617.8 2.2 convolution_subtract_fusion.7
  626.4 1.1 convolution_subtract_fusion.11
  628.1 1.2 convolution_subtract_fusion.3
  630.3 16.7 %fusion.4 = f32[1,512,2048]{2,1,0:T(8,128)} fusion(f32[1,2048,2048]{2,1,0:T(8,128)} %param.5, s32[]{:T(128)S(6)} %select_n.20, f32[1024,512]{1,0:T(8,128)S(1)} %constant_dynamic-update-slice_fusion.36, f32[1024,2048]{1,0:T(8,128)S(1)} %bitcast.174), kind=kOutput, calls=%fused_computation.9 | convolution fusion | flops 12885950464 | bytes 18874372 | tf_op jit(solution)/shard_map/dot_general | solution.py:44
  647.0 1.3 copy.83
  (106 shorter events, 29.2 us)
Async XLA Ops:
  7.2 171.3 %all-gather.6.cloned.1.call-start = ((), (), s32[]{:S(2)}) async-start(), calls=%async_computation.3 | async-start | bytes 10485760 | tf_op jit(solution)/shard_map/all_gather | solution.py:31
  64.3 18.8 %copy-start = (f32[8,32,2048]{2,0,1:T(8,128)}, f32[8,32,2048]{2,0,1:T(8,128)S(1)}, u32[]{:S(2)}) copy-start(f32[8,32,2048]{2,0,1:T(8,128)S(1)} %all_to_all.30) | copy-start | bytes 6291460
  83.1 167.0 %all-gather.4.cloned.1.call-start = ((), (), s32[]{:S(2)}) async-start(), calls=%async_computation.2 | async-start | bytes 10485760 | tf_op jit(solution)/shard_map/all_gather | solution.py:30
  83.8 94.6 %all-to-all-start.1 = ((f32[32,8,1,2048]{3,1,2,0:T(8,128)}), f32[32,8,1,2048]{3,1,2,0:T(8,128)S(1)}, u32[]{:S(2)}, u32[]{:S(2)}) async-start(f32[32,8,1,2048]{3,1,2,0:T(8,128)} %bitcast.6), calls=%async_computation.1 | async-start | bytes 4194304 | tf_op jit(solution)/shard_map/all_to_all | solution.py:45
  292.5 2.0 copy-start.2
  604.9 3.9 copy-start.1
  626.3 3.6 slice-start
  628.0 2.3 slice-start.1
Sparse Core Ops, SparseCore 0:
  83.2 80.5 all-gather.5
  166.0 84.0 all-gather.3
where the time goes:
time: 664 us; the launch traced here: 656 us
  other arithmetic  260 us (39%)
  blocking collectives  127 us (19%)
  matrix products  121 us (18%)
  waiting for transfers between devices  72.4 us (11%)
  local copies, waits for them, and re-layouts  49.4 us (7%)
  between operations  20.3 us (3%)
    another operation x30, other arithmetic, body(): cholesky_factor = jnp.linalg.cholesky(capacitance)  172 us
    another operation x3, other arithmetic, body(): solved = jax.scipy.linalg.cho_solve((cholesky_factor, True), white_block)  83.7 us
    psum x1, blocking collectives, body(): lev_send = lax.psum(lev_terms, 'dev') / (num_dev * feat_width)  81.7 us
    all_gather x1, waiting for transfers between devices, body(): lax.all_gather(own_rows, 'rep', axis=0, tiled=True)  71.6 us
    all_to_all x1, blocking collectives, body(): lax.all_to_all(features, 'dev', split_axis=1, concat_axis=0, tiled=True)  37.5 us
    dot_general x1, matrix products, body(): jnp.dot(all_rows, all_white.T, precision=lax.Precision.HIGHEST)  32.1 us
    another operation x30, matrix products, body(): solved = jax.scipy.linalg.cho_solve((cholesky_factor, True), white_block)  25.2 us
    another operation x14, matrix products, body(): cholesky_factor = jnp.linalg.cholesky(capacitance)  22.9 us
  transfers between devices with their start and end apart: 3, of which 1 were waited for; matrix products, arithmetic and copies ran while one was open for 0% of the time, Pallas kernels for 0%

commit v1 on v0

--- a/solution.py
+++ b/solution.py
@@ -20,7 +20,9 @@
         "etmo,etmi->emoi", grads_four, acts_four, preferred_element_type=jnp.float32
     )
     features = features.reshape(examples, num_dev, feat_width) * tokens ** (-0.5)
-    moved = lax.all_to_all(features, "dev", split_axis=1, concat_axis=0, tiled=True)
+    pieces = jnp.split(features, lax.axis_size("dev"), axis=1)
+    received = lax.all_to_all(jnp.stack(pieces), "dev", 0, 0)
+    moved = jnp.concatenate(received, axis=0)
     own_rows = moved[:, 0, :]
     module_inverse = inverse[0]
     whitened = jnp.dot(own_rows, module_inverse, precision=lax.Precision.HIGHEST)

time: 664 us -> 668 us (level)
    another operation x24 -> x25, local copies, waits for them, and re-layouts: 22.4 us -> 22.5 us
where the time goes in v1:
time: 668 us; the launch traced here: 658 us
  other arithmetic  260 us (39%)
  blocking collectives  127 us (19%)
  matrix products  122 us (18%)
  waiting for transfers between devices  70.2 us (11%)
  local copies, waits for them, and re-layouts  52.5 us (8%)
  between operations  20.5 us (3%)
    another operation x30, other arithmetic, body(): cholesky_factor = jnp.linalg.cholesky(capacitance)  172 us
    another operation x3, other arithmetic, body(): solved = jax.scipy.linalg.cho_solve((cholesky_factor, True), white_block)  83.7 us
    psum x1, blocking collectives, body(): lev_send = lax.psum(lev_terms, 'dev') / (num_dev * feat_width)  81.7 us
    all_gather x1, waiting for transfers between devices, body(): lax.all_gather(own_rows, 'rep', axis=0, tiled=True)  70.1 us
    all_to_all x1, blocking collectives, body(): received = lax.all_to_all(jnp.stack(pieces), 'dev', 0, 0)  37.5 us
    dot_general x1, matrix products, body(): jnp.dot(all_rows, all_white.T, precision=lax.Precision.HIGHEST)  32.1 us
    another operation x30, matrix products, body(): solved = jax.scipy.linalg.cho_solve((cholesky_factor, True), white_block)  25.2 us
    another operation x14, matrix products, body(): cholesky_factor = jnp.linalg.cholesky(capacitance)  22.9 us
  transfers between devices with their start and end apart: 3, of which 1 were waited for; matrix products, arithmetic and copies ran while one was open for 0% of the time, Pallas kernels for 0%

profile of v1, /device:TPU:1, one launch (start us, length us, event | category | flops | bytes accessed | tf_op | source)
XLA Modules:
  0.0 657.7 jit_solution(2649103576879779104)
XLA Ops:
  7.2 2.0 copy.12
  9.2 7.1 %reshape.130 = bf16[8,64,32,64]{3,2,1,0:T(8,128)(2,1)} reshape(bf16[1,8,64,2048]{3,2,1,0:T(8,128)(2,1)} %param.3) | data formatting | bytes 4194304 | tf_op jit(solution)/shard_map/reshape | solution.py:17
  16.3 5.6 fusion.7
  21.9 3.6 mul.29
  27.8 37.5 %all_to_all.20 = f32[32,8,1,2048]{3,2,1,0:T(1,128)S(1)} all-to-all(f32[32,8,1,2048]{3,2,1,0:T(1,128)S(1)} %constant_dynamic-update-slice_fusion), channel_id=1, replica_groups=mesh['dev'=32,'rep'=4] {'dev'}, dimensions={0} | all-to-all | bytes 4194304 | tf_op jit(solution)/shard_map/all_to_all | solution.py:24
  65.3 19.9 %multiply_reduce_fusion = (f32[256]{0:T(256)S(1)}, f32[256,2048]{1,0:T(8,128)}) fusion(f32[32,8,1,2048]{3,2,1,0:T(1,128)S(1)} %all_to_all.20, f32[1,2048,2048]{2,1,0:T(8,128)} %param.5), kind=kOutput, calls=%fused_computation.17 | convolution fusion | flops 12885950464 | bytes 20972544 | tf_op jit(solution)/shard_map/dot_general | solution.py:28
  85.2 2.2 copy.27
  87.5 4.3 all-to-all-start.1
  91.8 81.7 %psum.7 = f32[256]{0:T(256)S(1)} all-reduce(f32[256]{0:T(256)S(1)} %get-tuple-element.60), channel_id=1, replica_groups=mesh['dev'=32,'rep'=4] {'dev'}, use_global_device_ids=true, to_apply=%region_1.0 | all-reduce | flops 256 | bytes 2048 | tf_op jit(solution)/shard_map/psum | solution.py:30
  173.5 8.0 %all-gather = f32[4,1,256]{2,1,0:T(1,128)S(1)} all-gather(f32[1,1,256]{2,1,0:T(1,128)S(1)} %bitcast.305), channel_id=1, replica_groups=mesh['dev'=32,'rep'=4] {'rep'}, dimensions={0}, use_global_device_ids=true | all-gather | bytes 5120 | tf_op jit(solution)/shard_map/all_gather | solution.py:34
  182.1 70.1 %all-gather.4.cloned.1.call-done = f32[1024,2048]{1,0:T(8,128)} async-done(((f32[256,2048]{1,0:T(8,128)}), f32[1024,2048]{1,0:T(8,128)}) %all-gather.4.cloned.1.call-update) | async-done | bytes 8388624 | tf_op jit(solution)/shard_map/all_gather | solution.py:32
  252.2 32.1 %fusion.105 = f32[1024,1024]{1,0:T(8,128)} fusion(f32[1024,2048]{1,0:T(8,128)} %all-gather.4.cloned.1.call-done, f32[1024,2048]{1,0:T(8,128)} %all-gather.6.cloned.1.call-done), kind=kOutput, calls=%fused_computation.293 | convolution fusion | flops 25769803776 | bytes 20971520 | tf_op jit(solution)/shard_map/dot_general | solution.py:37
  284.3 5.7 copy.15
  290.0 4.5 fusion.3
  294.6 2.0 copy-done.1
  296.6 11.7 %cholesky.222 = f32[128,128]{1,0:T(8,128)S(1)} custom-call(f32[128,128]{1,0:T(8,128)S(1)} %cholesky.577), custom_call_target="Cholesky" | custom-call | tf_op jit(solution)/shard_map/jit(cholesky)/cholesky | solution.py:40
  308.3 2.5 cholesky.254
  310.8 9.8 %custom-call.66 = f32[1,128,128]{1,2,0:T(8,128)S(1)} custom-call(f32[1,128,128]{2,1,0:T(8,128)S(1)} %get-tuple-element.59), custom_call_target="InvertDiagBlocksLowerTriangular" | custom-call | tf_op jit(solution)/shard_map/jit(cholesky)/cholesky | solution.py:40
  320.7 2.3 constant_dynamic-update-slice_fusion.80
  323.0 1.5 convolution_subtract_fusion
  324.5 11.8 %cholesky.243 = f32[128,128]{1,0:T(8,128)S(1)} custom-call(f32[128,128]{1,0:T(8,128)S(1)} %cholesky.581), custom_call_target="Cholesky" | custom-call | tf_op jit(solution)/shard_map/jit(cholesky)/cholesky | solution.py:40
  337.0 9.8 %custom-call.67 = f32[1,128,128]{1,2,0:T(8,128)S(1)} custom-call(f32[1,128,128]{2,1,0:T(8,128)S(1)} %get-tuple-element.56), custom_call_target="InvertDiagBlocksLowerTriangular" | custom-call | tf_op jit(solution)/shard_map/jit(cholesky)/cholesky | solution.py:40
  346.8 1.2 convolution_dynamic-update-slice_fusion
  348.0 2.1 convolution_subtract_fusion.1
  350.2 11.7 %cholesky.466 = f32[128,128]{1,0:T(8,128)S(1)} custom-call(f32[128,128]{1,0:T(8,128)S(1)} %cholesky.586), custom_call_target="Cholesky" | custom-call | tf_op jit(solution)/shard_map/jit(cholesky)/cholesky | solution.py:40
  362.5 9.8 %custom-call.68 = f32[1,128,128]{1,2,0:T(8,128)S(1)} custom-call(f32[1,128,128]{2,1,0:T(8,128)S(1)} %get-tuple-element.53), custom_call_target="InvertDiagBlocksLowerTriangular" | custom-call | tf_op jit(solution)/shard_map/jit(cholesky)/cholesky | solution.py:40
  372.3 1.1 convolution_dynamic-update-slice_fusion.1
  373.5 2.3 convolution_subtract_fusion.2
  375.8 11.9 %cholesky.485 = f32[128,128]{1,0:T(8,128)S(1)} custom-call(f32[128,128]{1,0:T(8,128)S(1)} %cholesky.591), custom_call_target="Cholesky" | custom-call | tf_op jit(solution)/shard_map/jit(cholesky)/cholesky | solution.py:40
  388.4 9.8 %custom-call.69 = f32[1,128,128]{1,2,0:T(8,128)S(1)} custom-call(f32[1,128,128]{2,1,0:T(8,128)S(1)} %get-tuple-element.50), custom_call_target="InvertDiagBlocksLowerTriangular" | custom-call | tf_op jit(solution)/shard_map/jit(cholesky)/cholesky | solution.py:40
  399.2 2.3 convolution_subtract_fusion.17
  401.6 11.7 %cholesky.504 = f32[128,128]{1,0:T(8,128)S(1)} custom-call(f32[128,128]{1,0:T(8,128)S(1)} %cholesky.596), custom_call_target="Cholesky" | custom-call | tf_op jit(solution)/shard_map/jit(cholesky)/cholesky | solution.py:40
  413.9 10.2 %custom-call.70 = f32[1,128,128]{1,2,0:T(8,128)S(1)} custom-call(f32[1,128,128]{2,1,0:T(8,128)S(1)} %get-tuple-element.47), custom_call_target="InvertDiagBlocksLowerTriangular" | custom-call | tf_op jit(solution)/shard_map/jit(cholesky)/cholesky | solution.py:40
  425.1 2.3 convolution_subtract_fusion.18
  427.4 11.7 %cholesky.524 = f32[128,128]{1,0:T(8,128)S(1)} custom-call(f32[128,128]{1,0:T(8,128)S(1)} %cholesky.601), custom_call_target="Cholesky" | custom-call | tf_op jit(solution)/shard_map/jit(cholesky)/cholesky | solution.py:40
  439.8 9.8 %custom-call.71 = f32[1,128,128]{1,2,0:T(8,128)S(1)} custom-call(f32[1,128,128]{2,1,0:T(8,128)S(1)} %get-tuple-element.44), custom_call_target="InvertDiagBlocksLowerTriangular" | custom-call | tf_op jit(solution)/shard_map/jit(cholesky)/cholesky | solution.py:40
  450.5 2.1 convolution_subtract_fusion.19
  452.6 11.9 %cholesky.544 = f32[128,128]{1,0:T(8,128)S(1)} custom-call(f32[128,128]{1,0:T(8,128)S(1)} %cholesky.606), custom_call_target="Cholesky" | custom-call | tf_op jit(solution)/shard_map/jit(cholesky)/cholesky | solution.py:40
  465.1 9.8 %custom-call.72 = f32[1,128,128]{1,2,0:T(8,128)S(1)} custom-call(f32[1,128,128]{2,1,0:T(8,128)S(1)} %get-tuple-element.41), custom_call_target="InvertDiagBlocksLowerTriangular" | custom-call | tf_op jit(solution)/shard_map/jit(cholesky)/cholesky | solution.py:40
  475.8 1.8 convolution_subtract_fusion.20
  477.6 11.7 %cholesky.562 = f32[128,128]{1,0:T(8,128)S(1)} custom-call(f32[128,128]{1,0:T(8,128)S(1)} %convolution_subtract_fusion.20), custom_call_target="Cholesky" | custom-call | tf_op jit(solution)/shard_map/jit(cholesky)/cholesky | solution.py:40
  499.3 4.9 select_select_fusion
  504.2 22.6 %while.1 = (s32[]{:T(128)}, f32[1024,1024]{1,0:T(8,128)}, s32[8,2]{0,1:T(2,128)S(1)}, f32[8,128,128]{2,1,0:T(8,128)S(1)}, s32[]{:T(128)}) while((s32[]{:T(128)}, f32[1024,1024]{1,0:T(8,128)}, s32[8,2]{0,1:T(2,128)S(1)}, f32[8,128,128]{2,1,0:T(8,128)S(1)}, s32[]{:T(128)}) %tuple.61), condition=%wide.while_cond, body=%wide.while_body.sunk | while | flops 2 | bytes 131189 | solution.py:44
  504.8 2.2 bitcast_dynamic-update-slice_fusion.2
  507.6 2.2 bitcast_dynamic-update-slice_fusion.2
  510.5 2.2 bitcast_dynamic-update-slice_fusion.2
  513.3 2.2 bitcast_dynamic-update-slice_fusion.2
  516.1 2.2 bitcast_dynamic-update-slice_fusion.2
  519.0 2.2 bitcast_dynamic-update-slice_fusion.2
  521.8 2.2 bitcast_dynamic-update-slice_fusion.2
  524.6 2.1 bitcast_dynamic-update-slice_fusion.2
  526.8 78.8 %custom-call.73 = f32[8,128,128]{1,2,0:T(8,128)S(1)} custom-call(f32[8,128,128]{2,1,0:T(8,128)S(1)} %get-tuple-element.10), custom_call_target="InvertDiagBlocksLowerTriangular" | custom-call | tf_op jit(solution)/shard_map/jit(_cho_solve)/triangular_solve | solution.py:44
  605.6 1.4 constant_dynamic-update-slice_fusion.42
  607.0 1.5 convolution_subtract_fusion.10
  609.0 1.5 convolution_subtract_fusion.9
  611.0 1.6 convolution_subtract_fusion.14
  613.0 1.7 convolution_subtract_fusion.16
  615.2 1.9 convolution_subtract_fusion.8
  617.5 2.0 convolution_subtract_fusion.13
  619.9 2.2 convolution_subtract_fusion.7
  628.5 1.1 convolution_subtract_fusion.11
  630.2 1.2 convolution_subtract_fusion.3
  632.4 16.7 %fusion.4 = f32[1,512,2048]{2,1,0:T(8,128)} fusion(f32[1,2048,2048]{2,1,0:T(8,128)} %param.5, s32[]{:T(128)S(6)} %select_n.20, f32[1024,512]{1,0:T(8,128)S(1)} %constant_dynamic-update-slice_fusion.68, f32[1024,2048]{1,0:T(8,128)S(1)} %bitcast.299), kind=kOutput, calls=%fused_computation.9 | convolution fusion | flops 12885950464 | bytes 18874372 | tf_op jit(solution)/shard_map/dot_general | solution.py:46
  649.1 1.3 copy.119
  (136 shorter events, 30.7 us)
Async XLA Ops:
  7.2 174.9 %all-gather.6.cloned.1.call-start = ((), (), s32[]{:S(2)}) async-start(), calls=%async_computation.3 | async-start | bytes 10485760 | tf_op jit(solution)/shard_map/all_gather | solution.py:33
  85.2 167.0 %all-gather.4.cloned.1.call-start = ((), (), s32[]{:S(2)}) async-start(), calls=%async_computation.2 | async-start | bytes 10485760 | tf_op jit(solution)/shard_map/all_gather | solution.py:32
  87.5 94.6 %all-to-all-start.1 = ((f32[32,8,1,2048]{3,1,2,0:T(8,128)}), f32[32,8,1,2048]{3,1,2,0:T(8,128)S(1)}, u32[]{:S(2)}, u32[]{:S(2)}) async-start(f32[32,8,1,2048]{3,1,2,0:T(8,128)} %bitcast.35), calls=%async_computation.1 | async-start | bytes 4194304 | tf_op jit(solution)/shard_map/all_to_all | solution.py:47
  294.6 2.0 copy-start.1
  607.0 3.9 copy-start
  628.4 3.6 slice-start
  630.1 2.3 slice-start.1
Sparse Core Ops, SparseCore 0:
  85.3 80.5 all-gather.5
  168.1 84.0 all-gather.3
